TPU v7x, 256 devices: a whole 4x4x8 slice. The times are simulated.
256 devices in a mesh: dp: 32 (over x, z), tensor: 8 (over y, core).
Axes of the slice: x: 4, y: 4, z: 8, core: 2. Of those that a mesh axis runs over, the one named last changes fastest.
Arguments:
- tubelets: bfloat16 [1024, 32, 4096], P('dp', 'tensor'), may hold values from -6 to 6
- keep_index: int32 [1024, 32], P('dp', 'tensor'), may hold values from -1 to 31, as said below
- dest_row: int32 [1024, 32], P('dp', 'tensor'), may hold values from -1 to 31, as said below
- dest_slot: int32 [1024, 32], P('dp', 'tensor'), may hold values from -1 to 1023, as said below
- segment: int32 [32, 1024], P('dp'), may hold values from -1 to 1023, as said below
- ln_gain: bfloat16 [4096], replicated, may hold values from 0.25 to 1.75
- w_query: bfloat16 [4096, 3072], P('dp', 'tensor')
- w_key: bfloat16 [4096, 3072], P('dp', 'tensor')
- w_value: bfloat16 [4096, 3072], P('dp', 'tensor'), may hold values from -0.09375 to 0.09375
Outputs:
- attended: bfloat16 [32, 1024, 3072], P('dp', None, 'tensor')
Inputs may be any that keep to these rules, and one draw needn't show every extreme that they name: `keep_index`: entry e of a clip's list belongs to tensor index e // 4 and, when kept, names a tubelet of that index's share, each at most once; -1 marks a dropped entry. Each share keeps 1 to 4 tubelets. `dest_row`: -1 exactly where keep_index is -1. A clip goes whole to one row; each row receives exactly one clip from each dp index, so at most 4 kept tubelets go from one device to one row; some dp index sends that many to every row. `dest_slot`: -1 exactly where keep_index is -1. A kept tubelet on tensor index j lands in slots j * 128 to (j + 1) * 128 - 1; no two kept tubelets share a row and a slot; some row has all its slots filled. `segment`: the clip whose tubelet fills each slot, clips numbered in the order of the tubelets array; -1 for an empty slot. Agrees with dest_row and dest_slot.
All inputs are finite; a program needn't handle non-finite values.
Results may differ from a plain program's by a relative error of at most 0.0082.
Values may be sent and summed in bfloat16 or wider, within the bound.
A program may use at most 64 MiB of HBM per device.

v0:
```python
import jax
import jax.numpy as jnp
from jax import lax
from jax.sharding import PartitionSpec as P

HS = 128
block_rows = 512


def layer_norm(values_in, ln_gain):
    floats = values_in.astype(jnp.float32)
    average = jnp.mean(floats, axis=-1, keepdims=True)
    centred = floats - average
    variance = jnp.mean(centred * centred, axis=-1, keepdims=True)
    return (centred * lax.rsqrt(variance + 1e-06) * ln_gain.astype(jnp.float32)).astype(
        jnp.bfloat16
    )


def bucket_targets(row_ids, is_kept, n_buckets, capacity):
    matches = (row_ids[:, None] == jnp.arange(n_buckets, dtype=jnp.int32)[None, :]).astype(
        jnp.int32
    )
    earlier = jnp.cumsum(matches, axis=0) - matches
    ranking = jnp.sum(earlier * matches, axis=1)
    return jnp.where(is_kept, row_ids * capacity + ranking, -1)


def invert(targets, first_vals, second_vals, count):
    matches = targets[None, :] == jnp.arange(count, dtype=jnp.int32)[:, None]
    present = jnp.any(matches, axis=1)
    first_pick = jnp.sum(jnp.where(matches, first_vals[None, :], 0), axis=1)
    second_pick = jnp.sum(jnp.where(matches, second_vals[None, :], 0), axis=1)
    return (present, first_pick, second_pick)


def pack_send(flat_rows, source_ids, row_ids, slot_ids, is_kept, n_buckets):
    entries = source_ids.shape[0]
    capacity = entries // n_buckets
    targets = bucket_targets(row_ids, is_kept, n_buckets, capacity)
    present, source_pick, slot_pick = invert(targets, source_ids, slot_ids, entries)
    send_rows = jnp.where(
        present[:, None], jnp.take(flat_rows, source_pick, axis=0), jnp.zeros((), flat_rows.dtype)
    )
    send_slots = jnp.where(present, slot_pick, -1)
    return (
        send_rows.reshape(n_buckets, capacity, flat_rows.shape[1]),
        send_slots.reshape(n_buckets, capacity),
    )


def place_rows(recv_rows, recv_slots, slot_count):
    flat_rows = recv_rows.reshape(-1, recv_rows.shape[-1])
    flat_slots = recv_slots.reshape(-1)
    positions = jnp.arange(flat_slots.shape[0], dtype=jnp.int32)
    present, picked, ignored = invert(flat_slots, positions, positions, slot_count)
    return jnp.where(
        present[:, None], jnp.take(flat_rows, picked, axis=0), jnp.zeros((), flat_rows.dtype)
    )


def attend(query_rows, key_rows, value_rows, seg_query, seg_key):
    scores = jnp.einsum("qhd,khd->hqk", query_rows, key_rows, preferred_element_type=jnp.float32)
    allowed = (seg_query[:, None] == seg_key[None, :]) & (seg_key[None, :] >= 0)
    masked = jnp.where(allowed[None], scores, -1e30)
    largest = jnp.max(masked, axis=-1, keepdims=True)
    weights = jnp.where(allowed[None], jnp.exp(masked - largest), 0.0)
    totals = jnp.sum(weights, axis=-1, keepdims=True)
    totals = jnp.where(totals > 0, totals, 1.0)
    weights_bf = (weights / totals).astype(jnp.bfloat16)
    mixed = jnp.einsum("hqk,khd->qhd", weights_bf, value_rows, preferred_element_type=jnp.float32)
    return mixed.astype(jnp.bfloat16)


def body(tubelets, keep_index, dest_row, dest_slot, segment, ln_gain, w_query, w_key, w_value):
    n_rows = lax.axis_size("dp")
    clip_count, share_len, width = tubelets.shape
    seg_ids = segment.reshape(-1)
    row_len = seg_ids.shape[0]
    tok_rows = row_len // lax.axis_size("tensor")
    width_cols = w_query.shape[1]
    heads_local = width_cols // HS
    column = lax.axis_index("tensor")
    is_kept = (keep_index >= 0).reshape(-1)
    local_ids = jnp.maximum(keep_index - column * share_len, 0)
    source_ids = (jnp.arange(clip_count, dtype=jnp.int32)[:, None] * share_len + local_ids).reshape(
        -1
    )
    local_slots = (dest_slot - column * tok_rows).reshape(-1)
    send_rows, send_slots = pack_send(
        tubelets.reshape(-1, width), source_ids, dest_row.reshape(-1), local_slots, is_kept, n_rows
    )
    recv_rows, recv_slots = (
        lax.all_to_all(send_rows, "dp", split_axis=0, concat_axis=0, tiled=True),
        lax.all_to_all(send_slots, "dp", split_axis=0, concat_axis=0, tiled=True),
    )
    normed_own = layer_norm(place_rows(recv_rows, recv_slots, tok_rows), ln_gain)
    normed_row = lax.all_gather(normed_own, "tensor", axis=0, tiled=True)
    pieces_in = (
        lax.all_gather(w_query, "dp", axis=0, tiled=True),
        lax.all_gather(w_key, "dp", axis=0, tiled=True),
        lax.all_gather(w_value, "dp", axis=0, tiled=True),
    )
    query_sum, key_sum, value_sum = tuple(
        (jnp.dot(normed_row, piece_w, preferred_element_type=jnp.float32) for piece_w in pieces_in)
    )
    query_rows = (query_sum * HS ** (-0.5)).astype(jnp.bfloat16)
    key_rows = key_sum.astype(jnp.bfloat16).reshape(row_len, heads_local, HS)
    value_rows = value_sum.astype(jnp.bfloat16).reshape(row_len, heads_local, HS)
    blocks = row_len // block_rows
    query_blocks = query_rows.reshape(blocks, block_rows, heads_local, HS)
    seg_blocks = seg_ids.reshape(blocks, block_rows)
    mixed = lax.map(
        lambda pair_in: attend(pair_in[0], key_rows, value_rows, pair_in[1], seg_ids),
        (query_blocks, seg_blocks),
    )
    return mixed.reshape(1, row_len, width_cols)


def solution(mesh):
    return jax.shard_map(
        body,
        mesh=mesh,
        in_specs=(
            P("dp", "tensor", None),
            P("dp", "tensor"),
            P("dp", "tensor"),
            P("dp", "tensor"),
            P("dp", None),
            P(),
            P("dp", "tensor"),
            P("dp", "tensor"),
            P("dp", "tensor"),
        ),
        out_specs=P("dp", None, "tensor"),
        check_vma=False,
    )
```

profile of v0, /device:TPU:8, one launch (start us, length us, event | category | flops | bytes accessed | tf_op | source)
XLA Modules:
  0.0 343.9 jit_solution(8539267349982979860)
XLA Ops:
  6.5 0.7 all-gather.7.cloned.1.call-update
  7.3 0.8 copy.40
  8.2 0.7 broadcast_compare_fusion.1
  9.1 0.7 maximum_add_fusion
  9.8 0.7 broadcast_subtract_fusion
  11.5 0.7 select_n.65
  12.2 11.3 %all-to-all-start = ((s32[32,1,4]{2,1,0:T(1,128)}), s32[32,1,4]{2,1,0:T(1,128)S(1)}, u32[]{:S(2)}, u32[]{:S(2)}) async-start(s32[32,1,4]{2,1,0:T(1,128)} %bitcast.5), calls=%async_computation | async-start | bytes 32768 | tf_op jit(solution)/shard_map/all_to_all | solution.py:95
  23.6 1.4 reshape.154
  25.0 1.2 gather_fusion
  26.4 1.2 reshape.155
  27.6 5.7 %all-to-all-done = s32[32,1,4]{2,1,0:T(1,128)S(1)} async-done(((s32[32,1,4]{2,1,0:T(1,128)}), s32[32,1,4]{2,1,0:T(1,128)S(1)}, u32[]{:S(2)}, u32[]{:S(2)}) %all-to-all-start) | async-done | bytes 544 | tf_op jit(solution)/shard_map/all_to_all | solution.py:95
  33.3 4.1 %all-to-all-start.1 = ((bf16[32,4,4096]{2,1,0:T(4,128)(2,1)}), bf16[32,4,4096]{2,1,0:T(4,128)(2,1)S(1)}, u32[]{:S(2)}, u32[]{:S(2)}) async-start(bf16[32,4,4096]{2,1,0:T(4,128)(2,1)} %reshape.155), calls=%async_computation.1 | async-start | bytes 2097152 | tf_op jit(solution)/shard_map/all_to_all | solution.py:94
  38.0 0.7 reduce.7
  39.1 28.2 %all-to-all-done.1 = bf16[32,4,4096]{2,1,0:T(4,128)(2,1)S(1)} async-done(((bf16[32,4,4096]{2,1,0:T(4,128)(2,1)}), bf16[32,4,4096]{2,1,0:T(4,128)(2,1)S(1)}, u32[]{:S(2)}, u32[]{:S(2)}) %all-to-all-start.1) | async-done | bytes 1048608 | tf_op jit(solution)/shard_map/all_to_all | solution.py:94
  67.5 1.2 gather_fusion.1
  69.7 1.5 fusion.32
  71.2 0.7 all-gather.9.cloned.1.call-update
  73.2 21.6 %all-gather.7.cloned.1.call-done = bf16[4096,384]{1,0:T(8,128)(2,1)} async-done(((bf16[128,384]{1,0:T(8,128)(2,1)}), bf16[4096,384]{1,0:T(8,128)(2,1)}) %all-gather.7.cloned.1.call-update) | async-done | bytes 3145744 | tf_op jit(solution)/shard_map/all_gather | solution.py:100
  94.8 50.0 %all-gather.5.cloned.1.call-done = bf16[1024,4096]{1,0:T(8,128)(2,1)} async-done(((bf16[128,4096]{1,0:T(8,128)(2,1)}), bf16[1024,4096]{1,0:T(8,128)(2,1)}) %all-gather.5.cloned.1.call-update) | async-done | bytes 8388624 | tf_op jit(solution)/shard_map/all_gather | solution.py:98
  144.8 8.7 %multiply_convert_fusion = bf16[1024,384]{1,0:T(8,128)(2,1)S(1)} fusion(bf16[1024,4096]{1,0:T(8,128)(2,1)} %all-gather.5.cloned.1.call-done, bf16[4096,384]{1,0:T(8,128)(2,1)} %all-gather.7.cloned.1.call-done), kind=kOutput, calls=%fused_computation.33 | convolution fusion | flops 3222011904 | bytes 12320768 | tf_op jit(solution)/shard_map/dot_general | solution.py:105
  154.1 73.7 %all-gather.9.cloned.1.call-done = bf16[4096,384]{1,0:T(8,128)(2,1)} async-done(((bf16[128,384]{1,0:T(8,128)(2,1)}), bf16[4096,384]{1,0:T(8,128)(2,1)}) %all-gather.9.cloned.1.call-update) | async-done | bytes 3145744 | tf_op jit(solution)/shard_map/all_gather | solution.py:101
  227.8 7.7 %convolution_convert_fusion.1 = bf16[1024,384]{0,1:T(8,128)(2,1)S(1)} fusion(bf16[1024,4096]{1,0:T(8,128)(2,1)} %all-gather.5.cloned.1.call-done, bf16[4096,384]{1,0:T(8,128)(2,1)} %all-gather.9.cloned.1.call-done), kind=kOutput, calls=%fused_computation.35 | convolution fusion | flops 3221618688 | bytes 12320768 | tf_op jit(solution)/shard_map/dot_general | solution.py:105
  235.9 70.4 %all-gather.11.cloned.1.call-done = bf16[4096,384]{1,0:T(8,128)(2,1)} async-done(((bf16[128,384]{1,0:T(8,128)(2,1)}), bf16[4096,384]{1,0:T(8,128)(2,1)}) %all-gather.11.cloned.1.call-update) | async-done | bytes 3145744 | tf_op jit(solution)/shard_map/all_gather | solution.py:102
  306.3 7.7 %convolution_convert_fusion = bf16[1024,384]{0,1:T(8,128)(2,1)S(1)} fusion(bf16[1024,4096]{1,0:T(8,128)(2,1)} %all-gather.5.cloned.1.call-done, bf16[4096,384]{1,0:T(8,128)(2,1)} %all-gather.11.cloned.1.call-done), kind=kOutput, calls=%fused_computation.34 | convolution fusion | flops 3221618688 | bytes 12320768 | tf_op jit(solution)/shard_map/dot_general | solution.py:105
  314.1 1.2 copy.47
  315.2 20.0 %while.10 = (s32[]{:T(128)}, bf16[2,512,3,128]{3,1,2,0:T(8,128)(2,1)S(1)}, s32[2,512]{1,0:T(2,128)S(1)}, s32[1,1024]{1,0:T(1,128)S(1)}, bf16[2,512,3,128]{3,1,2,...) while((s32[]{:T(128)}, ...), condition=%wide.region_12.14_spmd, body=%wide.region_9.13_spmd.sunk | while | flops 815993856 | bytes 16558177 | solution.py:113
  315.6 5.4 %fusion.58 = (f32[3,512]{1,0:T(4,128)S(1)}, f32[3,512,1024]{2,1,0:T(8,128)}) fusion(pred[512,1024]{1,0:T(8,128)(4,1)S(1)} %compare_and_fusion.4, bf16[1024,3,128]{2,0,1:T(8,128)(2,1)S(1)} %get-tuple-element.160, bf16[2,512,3,128]{3,1,2,0:T(8,128)(2,1)S(1)} %get-tuple-element.159, s32[]{:T(128)} %get-tuple-element.147), kind=kOutput, calls=%fused_computation.62.clone.1 | convolution fusion | flops 408945664 | bytes 8525828 | tf_op jit(solution)/shard_map/while/body/eval_jaxpr/sub | solution.py:67
  321.1 4.1 %fusion.59 = bf16[2,512,3,128]{3,1,2,0:T(8,128)(2,1)S(1)} fusion(bf16[2,512,3,128]{3,1,2,0:T(8,128)(2,1)S(1)} %get-tuple-element.148, s32[]{:T(128)} %get-tuple-element.147, bf16[1024,3,128]{2,0,1:T(8,128)(2,1)} %get-tuple-element.161, f32[3,512,1024]{2,1,0:T(8,128)} %get-tuple-element.137, f32[3,512]{1,0:T(4,128)S(1)} %compare_select_fusion.4), kind=kOutput, calls=%fused_computation.13.clone.1 | convolution fusion | flops 405995520 | bytes 7479300 | tf_op jit(solution)/shard_map/while/body/eval_jaxpr/hqk,khd->qhd/dot_general | solution.py:71
  325.7 5.4 %fusion.58 = (f32[3,512]{1,0:T(4,128)S(1)}, f32[3,512,1024]{2,1,0:T(8,128)}) fusion(pred[512,1024]{1,0:T(8,128)(4,1)S(1)} %compare_and_fusion.4, bf16[1024,3,128]{2,0,1:T(8,128)(2,1)S(1)} %get-tuple-element.160, bf16[2,512,3,128]{3,1,2,0:T(8,128)(2,1)S(1)} %get-tuple-element.159, s32[]{:T(128)} %get-tuple-element.147), kind=kOutput, calls=%fused_computation.62.clone.1 | convolution fusion | flops 408945664 | bytes 8525828 | tf_op jit(solution)/shard_map/while/body/eval_jaxpr/sub | solution.py:67
  331.1 4.1 %fusion.59 = bf16[2,512,3,128]{3,1,2,0:T(8,128)(2,1)S(1)} fusion(bf16[2,512,3,128]{3,1,2,0:T(8,128)(2,1)S(1)} %get-tuple-element.148, s32[]{:T(128)} %get-tuple-element.147, bf16[1024,3,128]{2,0,1:T(8,128)(2,1)} %get-tuple-element.161, f32[3,512,1024]{2,1,0:T(8,128)} %get-tuple-element.137, f32[3,512]{1,0:T(4,128)S(1)} %compare_select_fusion.4), kind=kOutput, calls=%fused_computation.13.clone.1 | convolution fusion | flops 405995520 | bytes 7479300 | tf_op jit(solution)/shard_map/while/body/eval_jaxpr/hqk,khd->qhd/dot_general | solution.py:71
  335.2 0.7 copy.52
  335.9 1.4 reshape.184
  (56 shorter events, 6.8 us)
Async XLA Ops:
  6.5 88.2 %all-gather.7.cloned.1.call-start = ((), (), s32[]{:S(2)}) async-start(), calls=%async_computation.3 | async-start | bytes 3244032 | tf_op jit(solution)/shard_map/all_gather | solution.py:100
  12.2 21.1 %all-to-all-start = ((s32[32,1,4]{2,1,0:T(1,128)}), s32[32,1,4]{2,1,0:T(1,128)S(1)}, u32[]{:S(2)}, u32[]{:S(2)}) async-start(s32[32,1,4]{2,1,0:T(1,128)} %bitcast.5), calls=%async_computation | async-start | bytes 32768 | tf_op jit(solution)/shard_map/all_to_all | solution.py:95
  26.2 11.3 %copy-start.1 = (bf16[4096]{0:T(1024)(128)(2,1)S(1)}, bf16[4096]{0:T(1024)(128)(2,1)}, u32[]{:S(2)}) copy-start(bf16[4096]{0:T(1024)(128)(2,1)} %param.18) | copy-start | bytes 24580
  33.3 34.0 %all-to-all-start.1 = ((bf16[32,4,4096]{2,1,0:T(4,128)(2,1)}), bf16[32,4,4096]{2,1,0:T(4,128)(2,1)S(1)}, u32[]{:S(2)}, u32[]{:S(2)}) async-start(bf16[32,4,4096]{2,1,0:T(4,128)(2,1)} %reshape.155), calls=%async_computation.1 | async-start | bytes 2097152 | tf_op jit(solution)/shard_map/all_to_all | solution.py:94
  37.4 107.4 %all-gather.5.cloned.1.call-start = ((), (), s32[]{:S(2)}) async-start(), calls=%async_computation.2 | async-start | bytes 9437184 | tf_op jit(solution)/shard_map/all_gather | solution.py:98
  68.7 3.8 %copy-start = (s32[1,1024]{1,0:T(1,128)S(1)}, s32[1,1024]{1,0:T(1,128)}, u32[]{:S(2)}) copy-start(s32[1,1024]{1,0:T(1,128)} %param.17) | copy-start | bytes 12292
  71.2 156.6 %all-gather.9.cloned.1.call-start = ((), (), s32[]{:S(2)}) async-start(), calls=%async_computation.4 | async-start | bytes 3244032 | tf_op jit(solution)/shard_map/all_gather | solution.py:101
  71.9 234.4 %all-gather.11.cloned.1.call-start = ((), (), s32[]{:S(2)}) async-start(), calls=%async_computation.5 | async-start | bytes 3244032 | tf_op jit(solution)/shard_map/all_gather | solution.py:102
Sparse Core Ops, SparseCore 0:
  9.9 84.8 all-gather.6
  96.6 48.1 all-gather.4
  147.4 80.3 all-gather.8
  230.2 76.0 all-gather.10
where the time goes:
time: 344 us
  waiting for transfers between devices  252 us (73%)
  matrix products  43.3 us (13%)
  starting transfers between devices  15.5 us (5%)
  between operations  13.4 us (4%)
  local copies, waits for them, and re-layouts  12.3 us (4%)
  other arithmetic  7.78 us (2%)
    all_gather x1, waiting for transfers between devices, body(): lax.all_gather(w_key, 'dp', axis=0, tiled=True)  73.7 us
    all_gather x1, waiting for transfers between devices, body(): lax.all_gather(w_value, 'dp', axis=0, tiled=True)  70.4 us
    all_gather x1, waiting for transfers between devices, body(): normed_row = lax.all_gather(normed_own, 'tensor', axis=0, tiled=True)  50 us
    all_to_all x1, waiting for transfers between devices, body(): lax.all_to_all(send_rows, 'dp', split_axis=0, concat_axis=0, tiled=True)  28.2 us
    dot_general x3, matrix products, body(): jnp.dot(normed_row, piece_w, preferred_element_type=jnp.float32)  24.2 us
    all_gather x1, waiting for transfers between devices, body(): lax.all_gather(w_query, 'dp', axis=0, tiled=True)  21.6 us
    all_to_all x1, starting transfers between devices, body(): lax.all_to_all(send_slots, 'dp', split_axis=0, concat_axis=0, tiled=True)  11.3 us
    sub x2, matrix products, attend(): weights = jnp.where(allowed[None], jnp.exp(masked - largest), 0.0)  10.8 us
  transfers between devices with their start and end apart: 6, of which 6 were waited for; matrix products, arithmetic and copies ran while one was open for 9% of the time, Pallas kernels for 0%

commit v1 on v0

--- a/solution.py
+++ b/solution.py
@@ -97,7 +97,9 @@
     normed_own = layer_norm(place_rows(recv_rows, recv_slots, tok_rows), ln_gain)
     normed_row = lax.all_gather(normed_own, "tensor", axis=0, tiled=True)
     pieces_in = (
-        lax.all_gather(w_query, "dp", axis=0, tiled=True),
+        jnp.concatenate(
+            lax.all_to_all(jnp.stack([w_query] * lax.axis_size("dp")), "dp", 0, 0), axis=0
+        ),
         lax.all_gather(w_key, "dp", axis=0, tiled=True),
         lax.all_gather(w_value, "dp", axis=0, tiled=True),
     )

time: 344 us -> 322 us (0.936)
  waiting for transfers between devices: 252 us -> 221 us
  starting transfers between devices: 15.5 us -> 20.8 us
  local copies, waits for them, and re-layouts: 12.3 us -> 16.3 us
    all_to_all x0 -> x1, waiting for transfers between devices: none -> 74.2 us  [body(): lax.all_to_all(jnp.stack([w_query] * lax.axis_size('dp')), 'dp', 0, 0)]
    all_gather x1, waiting for transfers between devices: 50 us -> 0.01 us  [body(): normed_row = lax.all_gather(normed_own, 'tensor', axis=0, tiled=True)]
    all_gather x1, waiting for transfers between devices: 73.7 us -> 42.7 us  [body(): lax.all_gather(w_key, 'dp', axis=0, tiled=True)]
    all_gather x1 -> x0, waiting for transfers between devices: 21.6 us -> none  [body(): lax.all_gather(w_query, 'dp', axis=0, tiled=True)]
    all_to_all x0 -> x1, starting transfers between devices: none -> 5.06 us  [body(): lax.all_to_all(jnp.stack([w_query] * lax.axis_size('dp')), 'dp', 0, 0)]
  transfers between devices with their start and end apart: 6 -> 6, of which waited for: 6 -> 5; matrix products, arithmetic and copies ran while one was open for 9% -> 8% of each run, Pallas kernels for 0% -> 0%
where the time goes in v1:
time: 322 us
  waiting for transfers between devices  221 us (69%)
  matrix products  42.3 us (13%)
  starting transfers between devices  20.8 us (6%)
  local copies, waits for them, and re-layouts  16.3 us (5%)
  between operations  13.4 us (4%)
  other arithmetic  7.72 us (2%)
    all_to_all x1, waiting for transfers between devices, body(): lax.all_to_all(jnp.stack([w_query] * lax.axis_size('dp')), 'dp', 0, 0)  74.2 us
    all_gather x1, waiting for transfers between devices, body(): lax.all_gather(w_value, 'dp', axis=0, tiled=True)  70.6 us
    all_gather x1, waiting for transfers between devices, body(): lax.all_gather(w_key, 'dp', axis=0, tiled=True)  42.7 us
    all_to_all x1, waiting for transfers between devices, body(): lax.all_to_all(send_rows, 'dp', split_axis=0, concat_axis=0, tiled=True)  26.6 us
    dot_general x3, matrix products, body(): jnp.dot(normed_row, piece_w, preferred_element_type=jnp.float32)  23.3 us
    all_to_all x1, starting transfers between devices, body(): lax.all_to_all(send_slots, 'dp', split_axis=0, concat_axis=0, tiled=True)  11.3 us
    sub x2, matrix products, attend(): weights = jnp.where(allowed[None], jnp.exp(masked - largest), 0.0)  10.8 us
    dot_general x2, matrix products, attend(): jnp.einsum('hqk,khd->qhd', weights_bf, value_rows, preferred_element_type...  8.16 us
  transfers between devices with their start and end apart: 6, of which 5 were waited for; matrix products, arithmetic and copies ran while one was open for 8% of the time, Pallas kernels for 0%

profile of v1, /device:TPU:8, one launch (start us, length us, event | category | flops | bytes accessed | tf_op | source)
XLA Modules:
  0.0 321.6 jit_solution(9422289802705823007)
XLA Ops:
  6.5 0.8 copy.40
  7.9 0.7 broadcast_compare_fusion.1
  8.8 0.7 maximum_add_fusion
  9.7 0.7 broadcast_subtract_fusion
  10.8 0.7 select_n.65
  11.5 11.3 %all-to-all-start = ((s32[32,1,4]{2,1,0:T(1,128)}), s32[32,1,4]{2,1,0:T(1,128)S(1)}, u32[]{:S(2)}, u32[]{:S(2)}) async-start(s32[32,1,4]{2,1,0:T(1,128)} %bitcast.5), calls=%async_computation | async-start | bytes 32768 | tf_op jit(solution)/shard_map/all_to_all | solution.py:95
  22.9 1.3 reshape.159
  24.2 1.2 gather_fusion
  25.7 1.2 reshape.160
  26.9 5.7 %all-to-all-done = s32[32,1,4]{2,1,0:T(1,128)S(1)} async-done(((s32[32,1,4]{2,1,0:T(1,128)}), s32[32,1,4]{2,1,0:T(1,128)S(1)}, u32[]{:S(2)}, u32[]{:S(2)}) %all-to-all-start) | async-done | bytes 544 | tf_op jit(solution)/shard_map/all_to_all | solution.py:95
  32.6 4.1 %all-to-all-start.1 = ((bf16[32,4,4096]{2,1,0:T(4,128)(2,1)}), bf16[32,4,4096]{2,1,0:T(4,128)(2,1)S(1)}, u32[]{:S(2)}, u32[]{:S(2)}) async-start(bf16[32,4,4096]{2,1,0:T(4,128)(2,1)} %reshape.160), calls=%async_computation.1 | async-start | bytes 2097152 | tf_op jit(solution)/shard_map/all_to_all | solution.py:94
  38.3 26.6 %all-to-all-done.1 = bf16[32,4,4096]{2,1,0:T(4,128)(2,1)S(1)} async-done(((bf16[32,4,4096]{2,1,0:T(4,128)(2,1)}), bf16[32,4,4096]{2,1,0:T(4,128)(2,1)S(1)}, u32[]{:S(2)}, u32[]{:S(2)}) %all-to-all-start.1) | async-done | bytes 1048608 | tf_op jit(solution)/shard_map/all_to_all | solution.py:94
  65.2 1.2 gather_fusion.1
  67.3 1.5 fusion.32
  68.9 0.7 all-gather.6.cloned.1.call-update
  69.6 2.1 stack.2
  71.7 5.1 %all-to-all-start.2 = ((bf16[32,128,384]{2,1,0:T(8,128)(2,1)}), bf16[32,128,384]{2,1,0:T(8,128)(2,1)S(1)}, u32[]{:S(2)}, u32[]{:S(2)}) async-start(bf16[32,128,384]{2,1,0:T(8,128)(2,1)} %stack.2), calls=%async_computation.2 | async-start | bytes 6291456 | tf_op jit(solution)/shard_map/all_to_all | solution.py:101
  78.2 74.2 %all-to-all-done.2 = bf16[32,128,384]{2,1,0:T(8,128)(2,1)S(1)} async-done(((bf16[32,128,384]{2,1,0:T(8,128)(2,1)}), bf16[32,128,384]{2,1,0:T(8,128)(2,1)S(1)}, u32[]{:S(2)}, u32[]{:S(2)}) %all-to-all-start.2) | async-done | bytes 3145760 | tf_op jit(solution)/shard_map/all_to_all | solution.py:101
  152.3 7.9 %multiply_convert_fusion = bf16[1024,384]{1,0:T(8,128)(2,1)} fusion(bf16[1024,4096]{1,0:T(8,128)(2,1)} %all-gather.4.cloned.1.call-done, bf16[4096,384]{1,0:T(8,128)(2,1)S(1)} %bitcast.46), kind=kOutput, calls=%fused_computation.33 | convolution fusion | flops 3222011904 | bytes 12320768 | tf_op jit(solution)/shard_map/dot_general | solution.py:107
  160.2 2.4 reshape.189
  162.7 42.7 %all-gather.6.cloned.1.call-done = bf16[4096,384]{1,0:T(8,128)(2,1)} async-done(((bf16[128,384]{1,0:T(8,128)(2,1)}), bf16[4096,384]{1,0:T(8,128)(2,1)}) %all-gather.6.cloned.1.call-update) | async-done | bytes 3145744 | tf_op jit(solution)/shard_map/all_gather | solution.py:103
  205.4 7.7 %convolution_convert_fusion.1 = bf16[1024,384]{0,1:T(8,128)(2,1)S(1)} fusion(bf16[1024,4096]{1,0:T(8,128)(2,1)} %all-gather.4.cloned.1.call-done, bf16[4096,384]{1,0:T(8,128)(2,1)} %all-gather.6.cloned.1.call-done), kind=kOutput, calls=%fused_computation.35 | convolution fusion | flops 3221618688 | bytes 12320768 | tf_op jit(solution)/shard_map/dot_general | solution.py:107
  213.5 70.6 %all-gather.8.cloned.1.call-done = bf16[4096,384]{1,0:T(8,128)(2,1)} async-done(((bf16[128,384]{1,0:T(8,128)(2,1)}), bf16[4096,384]{1,0:T(8,128)(2,1)}) %all-gather.8.cloned.1.call-update) | async-done | bytes 3145744 | tf_op jit(solution)/shard_map/all_gather | solution.py:104
  284.1 7.7 %convolution_convert_fusion = bf16[1024,384]{0,1:T(8,128)(2,1)S(1)} fusion(bf16[1024,4096]{1,0:T(8,128)(2,1)} %all-gather.4.cloned.1.call-done, bf16[4096,384]{1,0:T(8,128)(2,1)} %all-gather.8.cloned.1.call-done), kind=kOutput, calls=%fused_computation.34 | convolution fusion | flops 3221618688 | bytes 12320768 | tf_op jit(solution)/shard_map/dot_general | solution.py:107
  291.8 1.2 copy.47
  293.0 19.9 %while.10 = (s32[]{:T(128)}, bf16[2,512,3,128]{3,1,2,0:T(8,128)(2,1)S(1)}, s32[2,512]{1,0:T(2,128)S(1)}, s32[1,1024]{1,0:T(1,128)S(1)}, bf16[2,512,3,128]{3,1,2,...) while((s32[]{:T(128)}, ...), condition=%wide.region_12.14_spmd, body=%wide.region_9.13_spmd.sunk | while | flops 815993856 | bytes 16558177 | solution.py:115
  293.4 5.4 %fusion.58 = (f32[3,512]{1,0:T(4,128)S(1)}, f32[3,512,1024]{2,1,0:T(8,128)}) fusion(pred[512,1024]{1,0:T(8,128)(4,1)S(1)} %compare_and_fusion.4, bf16[1024,3,128]{2,0,1:T(8,128)(2,1)S(1)} %get-tuple-element.160, bf16[2,512,3,128]{3,1,2,0:T(8,128)(2,1)S(1)} %get-tuple-element.159, s32[]{:T(128)} %get-tuple-element.147), kind=kOutput, calls=%fused_computation.62.clone.1 | convolution fusion | flops 408945664 | bytes 8525828 | tf_op jit(solution)/shard_map/while/body/eval_jaxpr/sub | solution.py:67
  298.9 4.1 %fusion.59 = bf16[2,512,3,128]{3,1,2,0:T(8,128)(2,1)S(1)} fusion(bf16[2,512,3,128]{3,1,2,0:T(8,128)(2,1)S(1)} %get-tuple-element.148, s32[]{:T(128)} %get-tuple-element.147, bf16[1024,3,128]{2,0,1:T(8,128)(2,1)} %get-tuple-element.161, f32[3,512,1024]{2,1,0:T(8,128)} %get-tuple-element.137, f32[3,512]{1,0:T(4,128)S(1)} %compare_select_fusion.4), kind=kOutput, calls=%fused_computation.13.clone.1 | convolution fusion | flops 405995520 | bytes 7479300 | tf_op jit(solution)/shard_map/while/body/eval_jaxpr/hqk,khd->qhd/dot_general | solution.py:71
  303.4 5.4 %fusion.58 = (f32[3,512]{1,0:T(4,128)S(1)}, f32[3,512,1024]{2,1,0:T(8,128)}) fusion(pred[512,1024]{1,0:T(8,128)(4,1)S(1)} %compare_and_fusion.4, bf16[1024,3,128]{2,0,1:T(8,128)(2,1)S(1)} %get-tuple-element.160, bf16[2,512,3,128]{3,1,2,0:T(8,128)(2,1)S(1)} %get-tuple-element.159, s32[]{:T(128)} %get-tuple-element.147), kind=kOutput, calls=%fused_computation.62.clone.1 | convolution fusion | flops 408945664 | bytes 8525828 | tf_op jit(solution)/shard_map/while/body/eval_jaxpr/sub | solution.py:67
  308.8 4.1 %fusion.59 = bf16[2,512,3,128]{3,1,2,0:T(8,128)(2,1)S(1)} fusion(bf16[2,512,3,128]{3,1,2,0:T(8,128)(2,1)S(1)} %get-tuple-element.148, s32[]{:T(128)} %get-tuple-element.147, bf16[1024,3,128]{2,0,1:T(8,128)(2,1)} %get-tuple-element.161, f32[3,512,1024]{2,1,0:T(8,128)} %get-tuple-element.137, f32[3,512]{1,0:T(4,128)S(1)} %compare_select_fusion.4), kind=kOutput, calls=%fused_computation.13.clone.1 | convolution fusion | flops 405995520 | bytes 7479300 | tf_op jit(solution)/shard_map/while/body/eval_jaxpr/hqk,khd->qhd/dot_general | solution.py:71
  312.9 0.7 copy.52
  313.6 1.4 reshape.190
  (60 shorter events, 7.1 us)
Async XLA Ops:
  11.5 21.1 %all-to-all-start = ((s32[32,1,4]{2,1,0:T(1,128)}), s32[32,1,4]{2,1,0:T(1,128)S(1)}, u32[]{:S(2)}, u32[]{:S(2)}) async-start(s32[32,1,4]{2,1,0:T(1,128)} %bitcast.5), calls=%async_computation | async-start | bytes 32768 | tf_op jit(solution)/shard_map/all_to_all | solution.py:95
  25.4 11.3 %copy-start.3 = (bf16[4096]{0:T(1024)(128)(2,1)S(1)}, bf16[4096]{0:T(1024)(128)(2,1)}, u32[]{:S(2)}) copy-start(bf16[4096]{0:T(1024)(128)(2,1)} %param.18) | copy-start | bytes 24580
  32.6 32.3 %all-to-all-start.1 = ((bf16[32,4,4096]{2,1,0:T(4,128)(2,1)}), bf16[32,4,4096]{2,1,0:T(4,128)(2,1)S(1)}, u32[]{:S(2)}, u32[]{:S(2)}) async-start(bf16[32,4,4096]{2,1,0:T(4,128)(2,1)} %reshape.160), calls=%async_computation.1 | async-start | bytes 2097152 | tf_op jit(solution)/shard_map/all_to_all | solution.py:94
  36.7 115.6 %all-gather.4.cloned.1.call-start = ((), (), s32[]{:S(2)}) async-start(), calls=%async_computation.3 | async-start | bytes 9437184 | tf_op jit(solution)/shard_map/all_gather | solution.py:98
  66.4 3.2 copy-start.2
  68.8 136.6 %all-gather.6.cloned.1.call-start = ((), (), s32[]{:S(2)}) async-start(), calls=%async_computation.4 | async-start | bytes 3244032 | tf_op jit(solution)/shard_map/all_gather | solution.py:103
  71.7 5.8 %copy-start.1 = (s32[1,1024]{1,0:T(1,128)S(1)}, s32[1,1024]{1,0:T(1,128)}, u32[]{:S(2)}) copy-start(s32[1,1024]{1,0:T(1,128)} %param.17) | copy-start | bytes 12292
  71.7 80.6 %all-to-all-start.2 = ((bf16[32,128,384]{2,1,0:T(8,128)(2,1)}), bf16[32,128,384]{2,1,0:T(8,128)(2,1)S(1)}, u32[]{:S(2)}, u32[]{:S(2)}) async-start(bf16[32,128,384]{2,1,0:T(8,128)(2,1)} %stack.2), calls=%async_computation.2 | async-start | bytes 6291456 | tf_op jit(solution)/shard_map/all_to_all | solution.py:101
  76.8 207.3 %all-gather.8.cloned.1.call-start = ((), (), s32[]{:S(2)}) async-start(), calls=%async_computation.5 | async-start | bytes 3244032 | tf_op jit(solution)/shard_map/all_gather | solution.py:104
  213.5 79.5 %copy-start = (bf16[2,512,3,128]{3,1,2,0:T(8,128)(2,1)S(1)}, bf16[2,512,3,128]{3,1,2,0:T(8,128)(2,1)}, u32[]{:S(2)}) copy-start(bf16[2,512,3,128]{3,1,2,0:T(8,128)(2,1)} %custom-call.4) | copy-start | bytes 2359300
Sparse Core Ops, SparseCore 0:
  68.9 47.8 all-gather.3
  119.5 85.8 all-gather.5
  208.0 76.0 all-gather.7
